TPU v7x, 256 devices: a whole 4x4x8 slice. The times are simulated.
256 devices in a mesh: seq: 16 (over z, core), head: 16 (over y, x).
Axes of the slice: x: 4, y: 4, z: 8, core: 2. Of those that a mesh axis runs over, the one named last changes fastest.
Arguments:
- queries: bfloat16 [6144, 16384], P('seq', 'head'), may hold values from -5 to 5
- keys: bfloat16 [6144, 1024], P('seq', 'head'), may hold values from -5 to 5
- values: bfloat16 [6144, 1024], P('seq', 'head'), may hold values from -6 to 6
- feat_q: bfloat16 [128, 128, 128], P('head'), may hold values from -0.5 to 0.5
- feat_k: bfloat16 [128, 128, 128], P('head'), may hold values from -0.5 to 0.5
Outputs:
- grad_feat_q: float32 [128, 128, 128], P('head')
- grad_feat_k: float32 [128, 128, 128], P('head')
All inputs are finite; a program needn't handle non-finite values.
Results may differ from a plain program's by a relative error of at most 0.02.
Values may be sent and summed in bfloat16 or wider, within the bound.
A program may use at most 128 MiB of HBM per device.

v0:
```python
import math
import jax
import jax.numpy as jnp
from jax import lax
from jax.sharding import PartitionSpec as P

HIGHEST_MODE = lax.Precision.HIGHEST
MASKED_SCORE = -1e30


def from_partner(block, axis, stride):
    count = lax.axis_size(axis)
    route = []
    for low in range(count):
        high = low | 1 << stride
        if high != low and high < count:
            route += [(low, high), (high, low)]
    return lax.ppermute(block, axis, route)


def in_one_piece(arrays, axis, dim, along):
    columns = [a.reshape(*a.shape[:along], -1) for a in arrays]
    both = jnp.concatenate(columns, axis=along)
    filled, at, done = (lax.all_gather(both, axis, axis=dim, tiled=True), 0, [])
    for a, column in zip(arrays, columns):
        piece = filled[..., at : at + column.shape[along]]
        done.append(piece.reshape(*piece.shape[:along], *a.shape[along:]))
        at += column.shape[along]
    return tuple(done)


def together(arrays, axis):
    vector, at, done = (jnp.concatenate([a.reshape(-1) for a in arrays]), 0, [])
    so_far = lax.psum(vector, axis)
    for a in arrays:
        done.append(so_far[at : at + a.size].reshape(a.shape))
        at += a.size
    return tuple(done)


def split_wide(entries):
    high = entries.astype(jnp.bfloat16)
    low = (entries - high.astype(jnp.float32)).astype(jnp.bfloat16)
    return (high, low)


def wide_left(form, wide, narrow):
    high, low = split_wide(wide)
    return jnp.einsum(form, high, narrow, preferred_element_type=jnp.float32) + jnp.einsum(
        form, low, narrow, preferred_element_type=jnp.float32
    )


def wide_right(form, narrow, wide):
    high, low = split_wide(wide)
    return jnp.einsum(form, narrow, high, preferred_element_type=jnp.float32) + jnp.einsum(
        form, narrow, low, preferred_element_type=jnp.float32
    )


def attend_block(
    running, query_half, query_pos, key_rows, value_rows, key_first, group_count, score_scale
):
    row_peak, row_total, summed = running
    half_rows = query_half.shape[0]
    key_count = key_rows.shape[0]
    head_dim = key_rows.shape[1] // group_count
    grouped = query_half.reshape(half_rows, group_count, -1, head_dim)
    key_heads = key_rows.reshape(key_count, group_count, head_dim)
    value_heads = value_rows.reshape(key_count, group_count, head_dim)
    scores = (
        jnp.einsum("rgjd,kgd->gjrk", grouped, key_heads, preferred_element_type=jnp.float32)
        * score_scale
    )
    scores = scores.reshape(row_peak.shape[0], half_rows, key_count)
    key_pos = key_first + jnp.arange(key_count, dtype=jnp.int32)
    allowed = (key_pos[None, :] <= query_pos[:, None])[None]
    new_peak = jnp.maximum(row_peak, jnp.max(jnp.where(allowed, scores, MASKED_SCORE), axis=-1))
    weights = jnp.exp(jnp.where(allowed, scores - new_peak[..., None], MASKED_SCORE))
    factor = jnp.exp(row_peak - new_peak)
    row_total = row_total * factor + jnp.sum(weights, axis=-1)
    rounded = weights.astype(jnp.bfloat16).reshape(group_count, -1, half_rows, key_count)
    mixture = jnp.einsum("gjrk,kgd->gjrd", rounded, value_heads, preferred_element_type=jnp.float32)
    summed = summed * factor[..., None] + mixture.reshape(summed.shape)
    return (new_peak, row_total, summed)


def body(queries, keys, values, feat_q, feat_k):
    row_count = queries.shape[0]
    heads_here = feat_q.shape[0]
    head_dim = feat_q.shape[1]
    seq_count = lax.axis_size("seq")
    seq_place = lax.axis_index("seq")
    head_place = lax.axis_index("head")
    key_value = jnp.stack((keys, values))
    partner = from_partner(key_value, "head", 0)
    upper_half = head_place // (1 << 0) % 2 == 1
    key_value = jnp.where(
        upper_half,
        jnp.concatenate((partner, key_value), axis=2),
        jnp.concatenate((key_value, partner), axis=2),
    )
    group_count = key_value.shape[2] // head_dim
    group_size = heads_here // group_count
    query_pos = seq_place * row_count + jnp.arange(row_count, dtype=jnp.int32)
    half_rows = row_count // 2
    query_halves = (queries[:half_rows], queries[half_rows:])
    pos_halves = (query_pos[:half_rows], query_pos[half_rows:])
    top_halves = (jnp.max(pos_halves[0]), jnp.max(pos_halves[1]))
    score_scale = head_dim ** (-0.5)
    start_half = (
        jnp.full((heads_here, half_rows), MASKED_SCORE, jnp.float32),
        jnp.zeros((heads_here, half_rows), jnp.float32),
        jnp.zeros((heads_here, half_rows, head_dim), jnp.float32),
    )
    shard_part = lax.all_gather(key_value, "seq", axis=1, tiled=True)
    part_rows = shard_part.shape[1]
    block_rows = math.gcd(part_rows, 512)

    def one_step(step_index, halves_state):
        offset = step_index * block_rows
        key_rows = lax.dynamic_slice_in_dim(shard_part[0], offset, block_rows, 0)
        value_rows = lax.dynamic_slice_in_dim(shard_part[1], offset, block_rows, 0)
        updated = []
        for half_index in range(2):

            def attend_half(current, half_index=half_index):
                return attend_block(
                    current,
                    query_halves[half_index],
                    pos_halves[half_index],
                    key_rows,
                    value_rows,
                    offset,
                    group_count,
                    score_scale,
                )

            def unchanged(current):
                return current

            updated.append(
                lax.cond(
                    top_halves[half_index] >= offset,
                    attend_half,
                    unchanged,
                    halves_state[half_index],
                )
            )
        return tuple(updated)

    finished = lax.fori_loop(0, part_rows // block_rows, one_step, (start_half, start_half))
    teacher_out = jnp.concatenate(
        [
            (finished[half_index][2] / finished[half_index][1][..., None]).astype(jnp.bfloat16)
            for half_index in range(2)
        ],
        axis=1,
    )
    key_local = key_value[0].reshape(row_count, group_count, head_dim)
    value_local = key_value[1].reshape(row_count, group_count, head_dim)
    query_local = queries.reshape(row_count, heads_here, head_dim)
    query_pre = jnp.einsum("rhd,hdf->hrf", query_local, feat_q, preferred_element_type=jnp.float32)
    key_pre = jnp.einsum(
        "rgd,gjdf->gjrf",
        key_local,
        feat_k.reshape(group_count, group_size, head_dim, -1),
        preferred_element_type=jnp.float32,
    ).reshape(heads_here, row_count, -1)
    feat_count = query_pre.shape[-1]
    query_feat = jax.nn.softplus(query_pre).astype(jnp.bfloat16)
    key_feat = jax.nn.softplus(key_pre).astype(jnp.bfloat16)
    block_state = jnp.einsum(
        "gjrf,rgd->gjfd",
        key_feat.reshape(group_count, group_size, row_count, -1),
        value_local,
        preferred_element_type=jnp.float32,
    ).reshape(heads_here, feat_count, head_dim)
    block_norm = jnp.sum(key_feat, axis=1, dtype=jnp.float32)
    zero_pair = (jnp.zeros_like(block_state), jnp.zeros_like(block_norm))
    take_shard_part = tuple(
        (
            part.astype(jnp.float32)
            for part in in_one_piece(
                (block_state[None].astype(jnp.bfloat16), block_norm[None].astype(jnp.bfloat16)),
                "seq",
                0,
                3,
            )
        )
    )
    part_count = take_shard_part[0].shape[0]
    chosen = jnp.arange(part_count, dtype=jnp.int32) < seq_place
    before_state = zero_pair[0] + jnp.sum(
        jnp.where(chosen[:, None, None, None], take_shard_part[0], 0.0), axis=0
    )
    before_norm = zero_pair[1] + jnp.sum(
        jnp.where(chosen[:, None, None], take_shard_part[1], 0.0), axis=0
    )
    causal = jnp.arange(row_count)[:, None] >= jnp.arange(row_count)[None, :]
    affinity = jnp.einsum("hrf,hsf->hrs", query_feat, key_feat, preferred_element_type=jnp.float32)
    masked = jnp.where(causal[None], affinity, 0.0)
    local_mix = jnp.einsum(
        "gjrs,sgd->gjrd",
        masked.astype(jnp.bfloat16).reshape(group_count, group_size, row_count, row_count),
        value_local,
        preferred_element_type=jnp.float32,
    ).reshape(heads_here, row_count, head_dim)
    numerator = wide_right("hrf,hfd->hrd", query_feat, before_state) + local_mix
    denominator = wide_right("hrf,hf->hr", query_feat, before_norm) + jnp.sum(masked, axis=-1)
    student = numerator / denominator[..., None]
    total_tokens = row_count * seq_count
    grad_out = 2.0 * (student - teacher_out.astype(jnp.float32)) / total_tokens
    grad_numer = grad_out / denominator[..., None]
    grad_denom = -jnp.sum(grad_out * student, axis=-1) / denominator
    back_state = wide_right("hrf,hrd->hfd", query_feat, grad_numer)
    back_norm = wide_right("hrf,hr->hf", query_feat, grad_denom)

    def take_upper(running, shard_part):
        part_count = shard_part[0].shape[0]
        chosen = jnp.arange(part_count, dtype=jnp.int32) > seq_place
        return (
            running[0]
            + jnp.sum(jnp.where(chosen[:, None, None, None], shard_part[0], 0.0), axis=0),
            running[1] + jnp.sum(jnp.where(chosen[:, None, None], shard_part[1], 0.0), axis=0),
        )

    after_state, after_norm = take_upper(
        zero_pair,
        (
            lax.all_gather(back_state[None].astype(jnp.bfloat16), "seq", axis=0, tiled=True).astype(
                jnp.float32
            ),
            lax.all_gather(back_norm[None].astype(jnp.bfloat16), "seq", axis=0, tiled=True).astype(
                jnp.float32
            ),
        ),
    )
    grad_aff = wide_left(
        "gjrd,sgd->gjrs",
        grad_numer.reshape(group_count, group_size, row_count, head_dim),
        value_local,
    ).reshape(heads_here, row_count, row_count)
    grad_aff = jnp.where(causal[None], grad_aff + grad_denom[..., None], 0.0)
    grad_qfeat = (
        jnp.einsum("hrd,hfd->hrf", grad_numer, before_state, precision=HIGHEST_MODE)
        + grad_denom[..., None] * before_norm[:, None, :]
        + wide_left("hrs,hsf->hrf", grad_aff, key_feat)
    )
    grad_kfeat = (
        wide_right(
            "sgd,gjfd->gjsf",
            value_local,
            after_state.reshape(group_count, group_size, feat_count, head_dim),
        ).reshape(heads_here, row_count, feat_count)
        + after_norm[:, None, :]
        + wide_left("hrs,hrf->hsf", grad_aff, query_feat)
    )
    grad_wq = wide_right("rhd,hrf->hdf", query_local, grad_qfeat * jax.nn.sigmoid(query_pre))
    grad_wk = wide_right(
        "rgd,gjrf->gjdf",
        key_local,
        (grad_kfeat * jax.nn.sigmoid(key_pre)).reshape(
            group_count, group_size, row_count, feat_count
        ),
    ).reshape(heads_here, head_dim, feat_count)
    return tuple(
        (
            part.astype(jnp.float32)
            for part in together(
                (grad_wq.astype(jnp.bfloat16), grad_wk.astype(jnp.bfloat16)), "seq"
            )
        )
    )


def solution(mesh):
    return jax.shard_map(
        body,
        mesh=mesh,
        in_specs=(
            P("seq", "head"),
            P("seq", "head"),
            P("seq", "head"),
            P("head", None, None),
            P("head", None, None),
        ),
        out_specs=(P("head", None, None), P("head", None, None)),
        check_vma=False,
    )
```

profile of v0, /device:TPU:1, one launch (start us, length us, event | category | flops | bytes accessed | tf_op | source)
XLA Modules:
  0.0 392.3 jit_solution(10411164082974506304)
XLA Ops:
  9.3 2.1 collective-permute-start
  11.4 3.4 collective-permute-done
  21.4 2.2 select_reduce_fusion.1
  23.7 38.1 %all-gather.8.cloned.1.call-done = bf16[2,6144,128]{2,1,0:T(8,128)(2,1)} async-done(((bf16[2,384,128]{2,1,0:T(8,128)(2,1)}), bf16[2,6144,128]{2,1,0:T(8,128)(2,1)}) %all-gather.8.cloned.1.call-update) | async-done | bytes 3145744 | tf_op jit(solution)/shard_map/all_gather | solution.py:116
  62.8 56.6 %while.23 = (s32[]{:T(128)}, f32[8,192]{1,0:T(8,128)S(1)}, f32[8,192]{1,0:T(8,128)S(1)}, f32[8,192,128]{2,1,0:T(8,128)}, f32[8,192]{1,0:T(8,128)S(1)}, /*index=5...) while((s32[]{:T(128)}, f32[8,192]{1,0:T(8,128)S(1)}, ...), condition=%wide.region_15.16_spmd, body=%wide.region_6.15_spmd.sunk | while | flops 823598080 | bytes 37431328 | solution.py:152
  64.0 2.1 fusion.153
  66.2 4.4 %conditional.4 = ((f32[8,192]{1,0:T(8,128)S(1)}, f32[8,192]{1,0:T(8,128)S(1)}, f32[8,192,128]{2,1,0:T(8,128)})) conditional(s32[]{:T(128)} %convert_element_type.400, (f32[8,192]{1,0:T(8,128)S(1)}, f32[8,192]{1,0:T(8,128)S(1)}, f32[8,192,128]{2,1,0:T(8,128)}) %tuple.74, (s32[]{:T(128)}, s32[192]{0:T(256)S(1)}, bf16[192,1024]{1,0:T(8,128)(2,1)S(1)}, ...), branch_computations={%region_7.7_spmd, %region_8.10_spmd} | conditional | flops 411799040 | bytes 18453340 | solution.py:143
  70.6 3.5 conditional.5
  75.3 2.1 fusion.153
  77.4 4.4 %conditional.4 = ((f32[8,192]{1,0:T(8,128)S(1)}, f32[8,192]{1,0:T(8,128)S(1)}, f32[8,192,128]{2,1,0:T(8,128)})) conditional(s32[]{:T(128)} %convert_element_type.400, (f32[8,192]{1,0:T(8,128)S(1)}, f32[8,192]{1,0:T(8,128)S(1)}, f32[8,192,128]{2,1,0:T(8,128)}) %tuple.74, (s32[]{:T(128)}, s32[192]{0:T(256)S(1)}, bf16[192,1024]{1,0:T(8,128)(2,1)S(1)}, ...), branch_computations={%region_7.7_spmd, %region_8.10_spmd} | conditional | flops 411799040 | bytes 18453340 | solution.py:143
  81.9 3.5 conditional.5
  86.6 2.1 fusion.153
  90.0 2.2 fusion.153
  93.5 2.1 fusion.153
  96.9 2.1 fusion.153
  100.3 2.1 fusion.153
  103.7 2.1 fusion.153
  107.1 2.1 fusion.153
  110.5 2.1 fusion.153
  113.9 2.1 fusion.153
  121.8 2.5 copy.124
  124.3 2.4 divide_convert_fusion
  126.7 4.6 %slice.72 = bf16[16,8,128,128]{2,1,3,0:T(8,128)(2,1)} slice(bf16[16,8,128,129]{2,1,3,0:T(8,128)(2,1)} %all-gather.6.cloned.1.call-done), slice={[0:16], [0:8], [0:128], [0:128]} | slice | bytes 8388608 | tf_op jit(solution)/shard_map/slice | solution.py:26
  131.2 6.7 %copy.186 = bf16[16,8,128,128]{3,2,1,0:T(8,128)(2,1)} copy(bf16[16,8,128,128]{2,1,3,0:T(8,128)(2,1)} %slice.72) | data formatting | bytes 8388608
  137.9 3.2 select_reduce_fusion
  147.3 2.8 fusion.128
  158.5 91.9 %all-gather.1 = bf16[128,128]{1,0:T(8,128)(2,1)S(1)} all-gather(bf16[8,128]{1,0:T(8,128)(2,1)S(1)} %add_convert_fusion), channel_id=3, replica_groups=mesh['seq'=16,'head'=16] {'seq'}, dimensions={0}, use_global_device_ids=true | all-gather | bytes 34816 | tf_op jit(solution)/shard_map/all_gather | solution.py:234
  250.5 4.7 %fusion.117 = f32[8,384,128]{2,1,0:T(8,128)S(1)} fusion(bf16[8,384,128]{2,1,0:T(8,128)(2,1)S(1)} %select_convert_fusion.2, f32[8,384,384]{1,2,0:T(8,128)} %copy-done.2), kind=kOutput, calls=%fused_computation.179 | convolution fusion | flops 306708480 | bytes 7077888 | tf_op jit(solution)/shard_map/hrs,hrf->hsf/dot_general | solution.py:49
  257.2 7.9 %all-gather.10.cloned.1.call-done = bf16[128,128,128]{2,1,0:T(8,128)(2,1)} async-done(((bf16[8,128,128]{2,1,0:T(8,128)(2,1)}), bf16[128,128,128]{2,1,0:T(8,128)(2,1)}) %all-gather.10.cloned.1.call-update) | async-done | bytes 4194320 | tf_op jit(solution)/shard_map/all_gather | solution.py:231
  265.1 3.2 fusion.48
  269.9 2.1 fusion.55
  274.2 108.8 %all-reduce.2.cloned.1.call-done = bf16[262144]{0:T(1024)(128)(2,1)} async-done(((bf16[262144]{0:T(1024)(128)(2,1)}), bf16[262144]{0:T(1024)(128)(2,1)}) %all-reduce.2.cloned.1.call-update) | async-done | bytes 524304 | tf_op jit(solution)/shard_map/psum | solution.py:34
  (181 shorter events, 53.4 us)
Async XLA Ops:
  7.2 10.8 %copy-start = (bf16[8,128,128]{2,1,0:T(8,128)(2,1)S(1)}, bf16[8,128,128]{2,1,0:T(8,128)(2,1)}, u32[]{:S(2)}) copy-start(bf16[8,128,128]{2,1,0:T(8,128)(2,1)} %param.15) | copy-start | bytes 786436
  7.2 9.3 %copy-start.5 = (bf16[384,1024]{1,0:T(8,128)(2,1)S(1)}, bf16[384,1024]{1,0:T(8,128)(2,1)}, u32[]{:S(2)}) copy-start(bf16[384,1024]{1,0:T(8,128)(2,1)} %param.11) | copy-start | bytes 2359300
  7.2 54.6 %all-gather.8.cloned.1.call-start = ((), (), s32[]{:S(2)}) async-start(), calls=%async_computation.1 | async-start | bytes 3342336 | tf_op jit(solution)/shard_map/all_gather | solution.py:116
  8.2 8.3 %copy-start.18 = (bf16[8,128,128]{2,1,0:T(8,128)(2,1)S(1)}, bf16[8,128,128]{2,1,0:T(8,128)(2,1)}, u32[]{:S(2)}) copy-start(bf16[8,128,128]{2,1,0:T(8,128)(2,1)} %param.14) | copy-start | bytes 786436
  9.3 5.5 %collective-permute-start = (bf16[2,384,64]{2,1,0:T(8,128)(2,1)S(1)}, bf16[2,384,64]{2,1,0:T(8,128)(2,1)S(1)}, u32[]{:S(2)}, u32[]{:S(2)}) collective-permute-start(bf16[2,384,64]{2,1,0:T(8,128)(2,1)S(1)} %pad_maximum_fusion.3), channel_id=1, source_target_pairs={{0,1},{1,0},{2,3},{3,2},{4,5},{5,4},{6,7},{7,6},{8,9},{9,8},{10,11... | collective-permute-start | bytes 294920 | tf_op jit(solution)/shard_map/ppermute | solution.py:18
  15.7 111.0 %all-gather.6.cloned.1.call-start = ((), (), s32[]{:S(2)}) async-start(), calls=%async_computation | async-start | bytes 4491264 | tf_op jit(solution)/shard_map/all_gather | solution.py:24
  17.0 2.2 copy-start.3
  17.0 1.1 copy-start.8
  19.2 1.2 copy-start.14
  19.2 2.2 copy-start.9
  21.2 243.9 %all-gather.10.cloned.1.call-start = ((), (), s32[]{:S(2)}) async-start(), calls=%async_computation.3 | async-start | bytes 4456448 | tf_op jit(solution)/shard_map/all_gather | solution.py:231
  67.1 1.1 copy-start.12
  69.7 0.9 copy-start.13
  78.4 1.2 copy-start.12
  81.0 0.9 copy-start.13
  119.5 0.9 copy-start.11
  141.8 2.4 copy-start.19
  142.2 1.9 copy-start.16
  142.3 1.9 copy-start.17
  147.0 236.0 %all-reduce.2.cloned.1.call-start = ((), (), s32[]{:S(2)}) async-start(), calls=%async_computation.2 | async-start | bytes 1048576 | tf_op jit(solution)/shard_map/psum | solution.py:34
  150.8 1.1 copy-start.10
  152.0 2.1 copy-start.2
  152.0 2.5 copy-start.4
  154.5 1.7 copy-start.6
  156.2 99.0 %slice-start = ((s8[4718592]{0:T(1024)(128)(4,1)}), s8[524288]{0:T(1024)(128)(4,1)S(1)}, s32[]{:S(2)}) async-start(s8[4718592]{0:T(1024)(128)(4,1)} %bitcast.271), calls=%async_computation.4 | async-start | bytes 1048576
  158.2 97.0 %slice-start.1 = ((s8[4718592]{0:T(1024)(128)(4,1)}), s8[4194304]{0:T(1024)(128)(4,1)S(1)}, s32[]{:S(2)}) async-start(s8[4718592]{0:T(1024)(128)(4,1)} %bitcast.271), calls=%async_computation.5 | async-start | bytes 8388608
  268.5 1.4 copy-start.7
  272.4 1.0 copy-start.15
  274.2 111.6 %copy-start.1 = (bf16[8,128,128]{2,1,0:T(8,128)(2,1)S(1)}, bf16[8,128,128]{2,1,0:T(8,128)(2,1)}, u32[]{:S(2)}) copy-start(bf16[8,128,128]{2,1,0:T(8,128)(2,1)} %param.15) | copy-start | bytes 786436
Sparse Core Ops, SparseCore 0:
  15.8 45.9 all-gather.7
  63.7 40.6 all-gather.5
  147.1 117.8 all-gather.9
  274.3 108.6 all-reduce.1
where the time goes:
time: 394 us; the launch traced here: 392 us
  waiting for transfers between devices  158 us (40%)
  blocking collectives  91.9 us (23%)
  local copies, waits for them, and re-layouts  53.3 us (14%)
  matrix products  36.4 us (9%)
  other arithmetic  20.1 us (5%)
  loops' own time  15.4 us (4%)
  between operations  14.2 us (4%)
    psum x1, waiting for transfers between devices, together(): so_far = lax.psum(vector, axis)  109 us
    all_gather x1, blocking collectives, body(): lax.all_gather(back_norm[None].astype(jnp.bfloat16), 'seq', axis=0, tiled...  91.9 us
    all_gather x1, waiting for transfers between devices, body(): shard_part = lax.all_gather(key_value, 'seq', axis=1, tiled=True)  38.1 us
    slice x12, local copies, waits for them, and re-layouts, one_step(): value_rows = lax.dynamic_slice_in_dim(shard_part[1], offset, block_rows, 0)  25.2 us
    another operation x1, loops' own time, body(): lax.fori_loop(0, part_rows // block_rows, one_step, (start_half, start_ha...  14.8 us
    unnamed x45, local copies, waits for them, and re-layouts  13.5 us
  transfers between devices with their start and end apart: 5, of which 4 were waited for; matrix products, arithmetic and copies ran while one was open for 18% of the time, Pallas kernels for 0%

commit v1 on v0

--- a/solution.py
+++ b/solution.py
@@ -113,7 +113,22 @@
         jnp.zeros((heads_here, half_rows), jnp.float32),
         jnp.zeros((heads_here, half_rows, head_dim), jnp.float32),
     )
-    shard_part = lax.all_gather(key_value, "seq", axis=1, tiled=True)
+    ways, here, step = (lax.axis_size("seq"), lax.axis_index("seq"), key_value.shape[1])
+    dims = [n * ways if d == 1 else n for d, n in enumerate(key_value.shape)]
+    shard_part = lax.dynamic_update_slice_in_dim(
+        jnp.zeros(dims, key_value.dtype), key_value, here * step, axis=1
+    )
+    going_up = going_down = key_value
+    for far in range(1, ways // 2 + 1):
+        going_up = lax.ppermute(going_up, "seq", [(d, (d + 1) % ways) for d in range(ways)])
+        shard_part = lax.dynamic_update_slice_in_dim(
+            shard_part, going_up, (here - far) % ways * step, axis=1
+        )
+        if 2 * far < ways:
+            going_down = lax.ppermute(going_down, "seq", [(d, (d - 1) % ways) for d in range(ways)])
+            shard_part = lax.dynamic_update_slice_in_dim(
+                shard_part, going_down, (here + far) % ways * step, axis=1
+            )
     part_rows = shard_part.shape[1]
     block_rows = math.gcd(part_rows, 512)
 

time: 394 us -> 458 us (1.16)
  blocking collectives: 91.9 us -> 137 us
  starting transfers between devices: 2.68 us -> 46.7 us
  waiting for transfers between devices: 158 us -> 128 us
  local copies, waits for them, and re-layouts: 53.3 us -> 33.7 us
  matrix products: 36.4 us -> 51.1 us
  other arithmetic: 20.1 us -> 25.4 us
    all_gather x1, blocking collectives: 91.9 us -> 137 us  [body(): lax.all_gather(back_norm[None].astype(jnp.bfloat16), 'seq', axis=0, tiled...]
    ppermute x0 -> x15, starting transfers between devices: none -> 44.3 us  [the longest x7 41.7 us: body(): lax.ppermute(going_down, 'seq', [(d, (d - 1) % ways) for d in range(ways)])]
    all_gather x1 -> x0, waiting for transfers between devices: 38.1 us -> none  [body(): shard_part = lax.all_gather(key_value, 'seq', axis=1, tiled=True)]
    slice x12, local copies, waits for them, and re-layouts: 25.2 us -> 2.46 us  [one_step(): value_rows = lax.dynamic_slice_in_dim(shard_part[1], offset, block_rows, 0)]
    ppermute x0 -> x15, waiting for transfers between devices: none -> 12.6 us  [the longest x8 9.17 us: body(): lax.ppermute(going_up, 'seq', [(d, (d + 1) % ways) for d in range(ways)])]
    unnamed x45 -> x51, local copies, waits for them, and re-layouts: 13.5 us -> 12.1 us
  transfers between devices with their start and end apart: 5 -> 19, of which waited for: 4 -> 8; matrix products, arithmetic and copies ran while one was open for 18% -> 14% of each run, Pallas kernels for 0% -> 0%
where the time goes in v1:
time: 458 us; the launch traced here: 454 us
  blocking collectives  137 us (30%)
  waiting for transfers between devices  128 us (28%)
  matrix products  51.1 us (11%)
  starting transfers between devices  46.7 us (10%)
  local copies, waits for them, and re-layouts  33.7 us (7%)
  other arithmetic  25.4 us (6%)
  loops' own time  17.6 us (4%)
  between operations  14.5 us (3%)
    all_gather x1, blocking collectives, body(): lax.all_gather(back_norm[None].astype(jnp.bfloat16), 'seq', axis=0, tiled...  137 us
    psum x1, waiting for transfers between devices, together(): so_far = lax.psum(vector, axis)  109 us
    ppermute x7, starting transfers between devices, body(): lax.ppermute(going_down, 'seq', [(d, (d - 1) % ways) for d in range(ways)])  41.7 us
    another operation x1, loops' own time, body(): lax.fori_loop(0, part_rows // block_rows, one_step, (start_half, start_ha...  17 us
    unnamed x51, local copies, waits for them, and re-layouts  12.1 us
    ppermute x8, waiting for transfers between devices, body(): lax.ppermute(going_up, 'seq', [(d, (d + 1) % ways) for d in range(ways)])  9.17 us
  transfers between devices with their start and end apart: 19, of which 8 were waited for; matrix products, arithmetic and copies ran while one was open for 14% of the time, Pallas kernels for 0%

profile of v1, /device:TPU:1, one launch (start us, length us, event | category | flops | bytes accessed | tf_op | source)
XLA Modules:
  0.0 454.5 jit_solution(18057253395344388162)
XLA Ops:
  9.2 2.1 collective-permute-start
  13.4 2.0 fusion.126
  18.7 2.0 constant_dynamic-update-slice_fusion.15
  23.2 2.9 fusion.123
  27.3 2.0 fusion.71
  30.1 4.2 select_reduce_fusion.1
  34.3 3.5 collective-permute-start.4
  39.7 5.9 %collective-permute-start.6 = (bf16[2,384,128]{2,1,0:T(8,128)(2,1)S(1)}, bf16[2,384,128]{2,1,0:T(8,128)(2,1)S(1)}, u32[]{:S(2)}, u32[]{:S(2)}) collective-permute-start(bf16[2,384,128]{2,1,0:T(8,128)(2,1)S(1)} %collective-permute-done.4), channel_id=1, source_target_pairs={{0,240},{16,0},{32,16},{48,32},{64,48},{80,64},{96,80},{112,96},{1... | collective-permute-start | bytes 589832 | tf_op jit(solution)/shard_map/ppermute | solution.py:128
  46.7 9.2 %collective-permute-start.8 = (bf16[2,384,128]{2,1,0:T(8,128)(2,1)S(1)}, bf16[2,384,128]{2,1,0:T(8,128)(2,1)S(1)}, u32[]{:S(2)}, u32[]{:S(2)}) collective-permute-start(bf16[2,384,128]{2,1,0:T(8,128)(2,1)S(1)} %collective-permute-done.6), channel_id=1, source_target_pairs={{0,240},{16,0},{32,16},{48,32},{64,48},{80,64},{96,80},{112,96},{1... | collective-permute-start | bytes 589832 | tf_op jit(solution)/shard_map/ppermute | solution.py:128
  57.0 9.6 %collective-permute-start.10 = (bf16[2,384,128]{2,1,0:T(8,128)(2,1)S(1)}, bf16[2,384,128]{2,1,0:T(8,128)(2,1)S(1)}, u32[]{:S(2)}, u32[]{:S(2)}) collective-permute-start(bf16[2,384,128]{2,1,0:T(8,128)(2,1)S(1)} %collective-permute-done.8), channel_id=1, source_target_pairs={{0,240},{16,0},{32,16},{48,32},{64,48},{80,64},{96,80},{112,96},{1... | collective-permute-start | bytes 589832 | tf_op jit(solution)/shard_map/ppermute | solution.py:128
  67.7 6.8 %collective-permute-start.12 = (bf16[2,384,128]{2,1,0:T(8,128)(2,1)S(1)}, bf16[2,384,128]{2,1,0:T(8,128)(2,1)S(1)}, u32[]{:S(2)}, u32[]{:S(2)}) collective-permute-start(bf16[2,384,128]{2,1,0:T(8,128)(2,1)S(1)} %collective-permute-done.10), channel_id=1, source_target_pairs={{0,240},{16,0},{32,16},{48,32},{64,48},{80,64},{96,80},{112,96},{1... | collective-permute-start | bytes 589832 | tf_op jit(solution)/shard_map/ppermute | solution.py:128
  75.5 5.2 %collective-permute-start.14 = (bf16[2,384,128]{2,1,0:T(8,128)(2,1)S(1)}, bf16[2,384,128]{2,1,0:T(8,128)(2,1)S(1)}, u32[]{:S(2)}, u32[]{:S(2)}) collective-permute-start(bf16[2,384,128]{2,1,0:T(8,128)(2,1)S(1)} %collective-permute-done.12), channel_id=1, source_target_pairs={{0,240},{16,0},{32,16},{48,32},{64,48},{80,64},{96,80},{112,96},{1... | collective-permute-start | bytes 589832 | tf_op jit(solution)/shard_map/ppermute | solution.py:128
  80.8 4.0 collective-permute-done.13
  86.0 5.2 %collective-permute-done.15 = bf16[2,384,128]{2,1,0:T(8,128)(2,1)S(1)} collective-permute-done((bf16[2,384,128]{2,1,0:T(8,128)(2,1)S(1)}, bf16[2,384,128]{2,1,0:T(8,128)(2,1)S(1)}, u32[]{:S(2)}, u32[]{:S(2)}) %collective-permute-start.15) | collective-permute-done | bytes 196640 | tf_op jit(solution)/shard_map/ppermute | solution.py:123
  93.1 44.4 %while.23 = (s32[]{:T(128)}, f32[8,192]{1,0:T(8,128)S(1)}, f32[8,192]{1,0:T(8,128)S(1)}, f32[8,192,128]{2,1,0:T(8,128)}, f32[8,192]{1,0:T(8,128)S(1)}, /*index=5...) while((s32[]{:T(128)}, f32[8,192]{1,0:T(8,128)S(1)}, ...), condition=%wide.region_15.16_spmd, body=%wide.region_6.15_spmd.sunk | while | flops 823598080 | bytes 43722840 | solution.py:167
  94.7 6.1 %conditional.4 = ((f32[8,192]{1,0:T(8,128)S(1)}, f32[8,192]{1,0:T(8,128)S(1)}, f32[8,192,128]{2,1,0:T(8,128)})) conditional(s32[]{:T(128)} %convert_element_type.400, (f32[8,192]{1,0:T(8,128)S(1)}, f32[8,192]{1,0:T(8,128)S(1)}, f32[8,192,128]{2,1,0:T(8,128)}) %tuple.75, (s32[]{:T(128)}, s32[192]{0:T(256)}, bf16[192,1024]{1,0:T(8,128)(2,1)}, ...), branch_computations={%region_7.7_spmd, %region_8.10_spmd} | conditional | flops 411799040 | bytes 18453340 | solution.py:158
  100.8 6.0 %conditional.5 = ((f32[8,192]{1,0:T(8,128)S(1)}, f32[8,192]{1,0:T(8,128)S(1)}, f32[8,192,128]{2,1,0:T(8,128)})) conditional(s32[]{:T(128)} %convert_element_type.401, (f32[8,192]{1,0:T(8,128)S(1)}, f32[8,192]{1,0:T(8,128)S(1)}, f32[8,192,128]{2,1,0:T(8,128)}) %tuple.77, (s32[]{:T(128)}, s32[192]{0:T(256)}, bf16[192,1024]{1,0:T(8,128)(2,1)}, ...), branch_computations={%region_11.11_spmd, %region_12.14_spmd} | conditional | flops 411799040 | bytes 18453340 | solution.py:158
  108.5 6.1 %conditional.4 = ((f32[8,192]{1,0:T(8,128)S(1)}, f32[8,192]{1,0:T(8,128)S(1)}, f32[8,192,128]{2,1,0:T(8,128)})) conditional(s32[]{:T(128)} %convert_element_type.400, (f32[8,192]{1,0:T(8,128)S(1)}, f32[8,192]{1,0:T(8,128)S(1)}, f32[8,192,128]{2,1,0:T(8,128)}) %tuple.75, (s32[]{:T(128)}, s32[192]{0:T(256)}, bf16[192,1024]{1,0:T(8,128)(2,1)}, ...), branch_computations={%region_7.7_spmd, %region_8.10_spmd} | conditional | flops 411799040 | bytes 18453340 | solution.py:158
  114.6 6.0 %conditional.5 = ((f32[8,192]{1,0:T(8,128)S(1)}, f32[8,192]{1,0:T(8,128)S(1)}, f32[8,192,128]{2,1,0:T(8,128)})) conditional(s32[]{:T(128)} %convert_element_type.401, (f32[8,192]{1,0:T(8,128)S(1)}, f32[8,192]{1,0:T(8,128)S(1)}, f32[8,192,128]{2,1,0:T(8,128)}) %tuple.77, (s32[]{:T(128)}, s32[192]{0:T(256)}, bf16[192,1024]{1,0:T(8,128)(2,1)}, ...), branch_computations={%region_11.11_spmd, %region_12.14_spmd} | conditional | flops 411799040 | bytes 18453340 | solution.py:158
  140.6 4.6 %slice.72 = bf16[16,8,128,128]{2,1,3,0:T(8,128)(2,1)} slice(bf16[16,8,128,129]{2,1,3,0:T(8,128)(2,1)} %all-gather.5.cloned.1.call-done), slice={[0:16], [0:8], [0:128], [0:128]} | slice | bytes 8388608 | tf_op jit(solution)/shard_map/slice | solution.py:26
  145.2 6.8 %copy.186 = bf16[16,8,128,128]{3,2,1,0:T(8,128)(2,1)} copy(bf16[16,8,128,128]{2,1,3,0:T(8,128)(2,1)} %slice.72) | data formatting | bytes 8388608
  152.0 3.3 select_reduce_fusion
  158.4 2.0 multiply_reduce_fusion
  162.5 2.8 fusion.128
  166.9 1.9 add_select_fusion
  174.7 137.2 %all-gather.1 = bf16[128,128]{1,0:T(8,128)(2,1)S(1)} all-gather(bf16[8,128]{1,0:T(8,128)(2,1)S(1)} %add_convert_fusion), channel_id=3, replica_groups=mesh['seq'=16,'head'=16] {'seq'}, dimensions={0}, use_global_device_ids=true | all-gather | bytes 34816 | tf_op jit(solution)/shard_map/all_gather | solution.py:249
  312.0 4.7 %fusion.117 = f32[8,384,128]{2,1,0:T(8,128)S(1)} fusion(bf16[8,384,128]{2,1,0:T(8,128)(2,1)S(1)} %copy-done.3, f32[8,384,384]{1,2,0:T(8,128)} %copy-done.2), kind=kOutput, calls=%fused_computation.195 | convolution fusion | flops 306708480 | bytes 7077888 | tf_op jit(solution)/shard_map/hrs,hrf->hsf/dot_general | solution.py:49
  316.7 2.0 fusion.113
  318.7 6.4 %all-gather.7.cloned.1.call-done = bf16[128,128,128]{2,1,0:T(8,128)(2,1)} async-done(((bf16[8,128,128]{2,1,0:T(8,128)(2,1)}), bf16[128,128,128]{2,1,0:T(8,128)(2,1)}) %all-gather.7.cloned.1.call-update) | async-done | bytes 4194320 | tf_op jit(solution)/shard_map/all_gather | solution.py:246
  325.1 3.2 fusion.48
  329.8 2.6 fusion.55
  336.1 109.1 %all-reduce.2.cloned.1.call-done = bf16[262144]{0:T(1024)(128)(2,1)} async-done(((bf16[262144]{0:T(1024)(128)(2,1)}), bf16[262144]{0:T(1024)(128)(2,1)}) %all-reduce.2.cloned.1.call-update) | async-done | bytes 524304 | tf_op jit(solution)/shard_map/psum | solution.py:34
  (238 shorter events, 71.6 us)
Async XLA Ops:
  7.2 16.0 %copy-start = (bf16[8,128,128]{2,1,0:T(8,128)(2,1)S(1)}, bf16[8,128,128]{2,1,0:T(8,128)(2,1)}, u32[]{:S(2)}) copy-start(bf16[8,128,128]{2,1,0:T(8,128)(2,1)} %param.15) | copy-start | bytes 786436
  7.2 8.2 %copy-start.6 = (bf16[384,1024]{1,0:T(8,128)(2,1)S(1)}, bf16[384,1024]{1,0:T(8,128)(2,1)}, u32[]{:S(2)}) copy-start(bf16[384,1024]{1,0:T(8,128)(2,1)} %param.11) | copy-start | bytes 2359300
  7.2 8.2 %copy-start.21 = (bf16[8,128,128]{2,1,0:T(8,128)(2,1)S(1)}, bf16[8,128,128]{2,1,0:T(8,128)(2,1)}, u32[]{:S(2)}) copy-start(bf16[8,128,128]{2,1,0:T(8,128)(2,1)} %param.14) | copy-start | bytes 786436
  7.2 133.4 %all-gather.5.cloned.1.call-start = ((), (), s32[]{:S(2)}) async-start(), calls=%async_computation | async-start | bytes 4491264 | tf_op jit(solution)/shard_map/all_gather | solution.py:24
  9.2 6.6 %copy-start.15 = (bf16[384,64]{1,0:T(8,128)(2,1)}, bf16[384,64]{1,0:T(8,128)(2,1)S(1)}, u32[]{:S(2)}) copy-start(bf16[384,64]{1,0:T(8,128)(2,1)S(1)} %copy.116) | copy-start | bytes 147460
  9.2 9.0 %collective-permute-start = (bf16[2,384,64]{2,1,0:T(8,128)(2,1)S(1)}, bf16[2,384,64]{2,1,0:T(8,128)(2,1)}, u32[]{:S(2)}, u32[]{:S(2)}) collective-permute-start(bf16[2,384,64]{2,1,0:T(8,128)(2,1)S(1)} %pad_maximum_fusion.3), channel_id=1, source_target_pairs={{0,1},{1,0},{2,3},{3,2},{4,5},{5,4},{6,7},{7,6},{8,9},{9,8},{10,11... | collective-permute-start | bytes 294920 | tf_op jit(solution)/shard_map/ppermute | solution.py:18
  15.8 2.4 copy-start.4
  15.9 2.8 copy-start.16
  20.7 13.6 %collective-permute-start.2 = (bf16[2,384,128]{2,1,0:T(8,128)(2,1)}, bf16[2,384,128]{2,1,0:T(8,128)(2,1)}, u32[]{:S(2)}, u32[]{:S(2)}) collective-permute-start(bf16[2,384,128]{2,1,0:T(8,128)(2,1)} %get-tuple-element.353), channel_id=1, source_target_pairs={{0,240},{16,0},{32,16},{48,32},{64,48},{80,64},{96,80},{112,96},{1... | collective-permute-start | bytes 589832 | tf_op jit(solution)/shard_map/ppermute | solution.py:128
  22.2 15.6 %collective-permute-start.1 = (bf16[2,384,128]{2,1,0:T(8,128)(2,1)}, bf16[2,384,128]{2,1,0:T(8,128)(2,1)}, u32[]{:S(2)}, u32[]{:S(2)}) collective-permute-start(bf16[2,384,128]{2,1,0:T(8,128)(2,1)} %get-tuple-element.353), channel_id=1, source_target_pairs={{0,16},{16,32},{32,48},{48,64},{64,80},{80,96},{96,112},{112,128},... | collective-permute-start | bytes 589832 | tf_op jit(solution)/shard_map/ppermute | solution.py:123
  27.3 2.8 copy-start.17
  30.0 295.1 %all-gather.7.cloned.1.call-start = ((), (), s32[]{:S(2)}) async-start(), calls=%async_computation.2 | async-start | bytes 4456448 | tf_op jit(solution)/shard_map/all_gather | solution.py:246
  34.3 5.5 %collective-permute-start.4 = (bf16[2,384,128]{2,1,0:T(8,128)(2,1)}, bf16[2,384,128]{2,1,0:T(8,128)(2,1)S(1)}, u32[]{:S(2)}, u32[]{:S(2)}) collective-permute-start(bf16[2,384,128]{2,1,0:T(8,128)(2,1)} %collective-permute-done.2), channel_id=1, source_target_pairs={{0,240},{16,0},{32,16},{48,32},{64,48},{80,64},{96,80},{112,96},{1... | collective-permute-start | bytes 589832 | tf_op jit(solution)/shard_map/ppermute | solution.py:128
  37.8 7.9 %collective-permute-start.3 = (bf16[2,384,128]{2,1,0:T(8,128)(2,1)}, bf16[2,384,128]{2,1,0:T(8,128)(2,1)S(1)}, u32[]{:S(2)}, u32[]{:S(2)}) collective-permute-start(bf16[2,384,128]{2,1,0:T(8,128)(2,1)} %collective-permute-done.1), channel_id=1, source_target_pairs={{0,16},{16,32},{32,48},{48,64},{64,80},{80,96},{96,112},{112,128},... | collective-permute-start | bytes 589832 | tf_op jit(solution)/shard_map/ppermute | solution.py:123
  39.7 7.0 %collective-permute-start.6 = (bf16[2,384,128]{2,1,0:T(8,128)(2,1)S(1)}, bf16[2,384,128]{2,1,0:T(8,128)(2,1)S(1)}, u32[]{:S(2)}, u32[]{:S(2)}) collective-permute-start(bf16[2,384,128]{2,1,0:T(8,128)(2,1)S(1)} %collective-permute-done.4), channel_id=1, source_target_pairs={{0,240},{16,0},{32,16},{48,32},{64,48},{80,64},{96,80},{112,96},{1... | collective-permute-start | bytes 589832 | tf_op jit(solution)/shard_map/ppermute | solution.py:128
  45.7 10.3 %collective-permute-start.5 = (bf16[2,384,128]{2,1,0:T(8,128)(2,1)S(1)}, bf16[2,384,128]{2,1,0:T(8,128)(2,1)S(1)}, u32[]{:S(2)}, u32[]{:S(2)}) collective-permute-start(bf16[2,384,128]{2,1,0:T(8,128)(2,1)S(1)} %collective-permute-done.3), channel_id=1, source_target_pairs={{0,16},{16,32},{32,48},{48,64},{64,80},{80,96},{96,112},{112,128},... | collective-permute-start | bytes 589832 | tf_op jit(solution)/shard_map/ppermute | solution.py:123
  46.7 10.3 %collective-permute-start.8 = (bf16[2,384,128]{2,1,0:T(8,128)(2,1)S(1)}, bf16[2,384,128]{2,1,0:T(8,128)(2,1)S(1)}, u32[]{:S(2)}, u32[]{:S(2)}) collective-permute-start(bf16[2,384,128]{2,1,0:T(8,128)(2,1)S(1)} %collective-permute-done.6), channel_id=1, source_target_pairs={{0,240},{16,0},{32,16},{48,32},{64,48},{80,64},{96,80},{112,96},{1... | collective-permute-start | bytes 589832 | tf_op jit(solution)/shard_map/ppermute | solution.py:128
  56.0 10.6 %collective-permute-start.7 = (bf16[2,384,128]{2,1,0:T(8,128)(2,1)S(1)}, bf16[2,384,128]{2,1,0:T(8,128)(2,1)S(1)}, u32[]{:S(2)}, u32[]{:S(2)}) collective-permute-start(bf16[2,384,128]{2,1,0:T(8,128)(2,1)S(1)} %collective-permute-done.5), channel_id=1, source_target_pairs={{0,16},{16,32},{32,48},{48,64},{64,80},{80,96},{96,112},{112,128},... | collective-permute-start | bytes 589832 | tf_op jit(solution)/shard_map/ppermute | solution.py:123
  57.0 10.7 %collective-permute-start.10 = (bf16[2,384,128]{2,1,0:T(8,128)(2,1)S(1)}, bf16[2,384,128]{2,1,0:T(8,128)(2,1)S(1)}, u32[]{:S(2)}, u32[]{:S(2)}) collective-permute-start(bf16[2,384,128]{2,1,0:T(8,128)(2,1)S(1)} %collective-permute-done.8), channel_id=1, source_target_pairs={{0,240},{16,0},{32,16},{48,32},{64,48},{80,64},{96,80},{112,96},{1... | collective-permute-start | bytes 589832 | tf_op jit(solution)/shard_map/ppermute | solution.py:128
  66.6 7.8 %collective-permute-start.9 = (bf16[2,384,128]{2,1,0:T(8,128)(2,1)S(1)}, bf16[2,384,128]{2,1,0:T(8,128)(2,1)S(1)}, u32[]{:S(2)}, u32[]{:S(2)}) collective-permute-start(bf16[2,384,128]{2,1,0:T(8,128)(2,1)S(1)} %collective-permute-done.7), channel_id=1, source_target_pairs={{0,16},{16,32},{32,48},{48,64},{64,80},{80,96},{96,112},{112,128},... | collective-permute-start | bytes 589832 | tf_op jit(solution)/shard_map/ppermute | solution.py:123
  67.7 7.8 %collective-permute-start.12 = (bf16[2,384,128]{2,1,0:T(8,128)(2,1)S(1)}, bf16[2,384,128]{2,1,0:T(8,128)(2,1)S(1)}, u32[]{:S(2)}, u32[]{:S(2)}) collective-permute-start(bf16[2,384,128]{2,1,0:T(8,128)(2,1)S(1)} %collective-permute-done.10), channel_id=1, source_target_pairs={{0,240},{16,0},{32,16},{48,32},{64,48},{80,64},{96,80},{112,96},{1... | collective-permute-start | bytes 589832 | tf_op jit(solution)/shard_map/ppermute | solution.py:128
  74.5 6.3 %collective-permute-start.11 = (bf16[2,384,128]{2,1,0:T(8,128)(2,1)S(1)}, bf16[2,384,128]{2,1,0:T(8,128)(2,1)S(1)}, u32[]{:S(2)}, u32[]{:S(2)}) collective-permute-start(bf16[2,384,128]{2,1,0:T(8,128)(2,1)S(1)} %collective-permute-done.9), channel_id=1, source_target_pairs={{0,16},{16,32},{32,48},{48,64},{64,80},{80,96},{96,112},{112,128},... | collective-permute-start | bytes 589832 | tf_op jit(solution)/shard_map/ppermute | solution.py:123
  75.5 10.4 %collective-permute-start.14 = (bf16[2,384,128]{2,1,0:T(8,128)(2,1)S(1)}, bf16[2,384,128]{2,1,0:T(8,128)(2,1)S(1)}, u32[]{:S(2)}, u32[]{:S(2)}) collective-permute-start(bf16[2,384,128]{2,1,0:T(8,128)(2,1)S(1)} %collective-permute-done.12), channel_id=1, source_target_pairs={{0,240},{16,0},{32,16},{48,32},{64,48},{80,64},{96,80},{112,96},{1... | collective-permute-start | bytes 589832 | tf_op jit(solution)/shard_map/ppermute | solution.py:128
  80.8 4.1 collective-permute-start.13
  84.8 6.3 %collective-permute-start.15 = (bf16[2,384,128]{2,1,0:T(8,128)(2,1)S(1)}, bf16[2,384,128]{2,1,0:T(8,128)(2,1)S(1)}, u32[]{:S(2)}, u32[]{:S(2)}) collective-permute-start(bf16[2,384,128]{2,1,0:T(8,128)(2,1)S(1)} %collective-permute-done.13), channel_id=1, source_target_pairs={{0,16},{16,32},{32,48},{48,64},{64,80},{80,96},{96,112},{112,128},... | collective-permute-start | bytes 589832 | tf_op jit(solution)/shard_map/ppermute | solution.py:123
  145.2 6.8 %copy-start.23 = (pred[16]{0:T(512)(128)(4,1)S(1)}, pred[16]{0:T(512)(128)(4,1)}, u32[]{:S(2)}) copy-start(pred[16]{0:T(512)(128)(4,1)} %iota_compare_fusion.2) | copy-start | bytes 52
  152.0 3.5 copy-start.3
  162.2 283.0 %all-reduce.2.cloned.1.call-start = ((), (), s32[]{:S(2)}) async-start(), calls=%async_computation.1 | async-start | bytes 1048576 | tf_op jit(solution)/shard_map/psum | solution.py:34
  168.9 2.6 copy-start.5
  173.1 143.6 %slice-start = ((s8[4718592]{0:T(1024)(128)(4,1)}), s8[524288]{0:T(1024)(128)(4,1)S(1)}, s32[]{:S(2)}) async-start(s8[4718592]{0:T(1024)(128)(4,1)} %bitcast.271), calls=%async_computation.3 | async-start | bytes 1048576
  174.5 142.3 %slice-start.1 = ((s8[4718592]{0:T(1024)(128)(4,1)}), s8[4194304]{0:T(1024)(128)(4,1)S(1)}, s32[]{:S(2)}) async-start(s8[4718592]{0:T(1024)(128)(4,1)} %bitcast.271), calls=%async_computation.4 | async-start | bytes 8388608
  333.7 114.2 %copy-start.1 = (bf16[8,128,128]{2,1,0:T(8,128)(2,1)S(1)}, bf16[8,128,128]{2,1,0:T(8,128)(2,1)}, u32[]{:S(2)}) copy-start(bf16[8,128,128]{2,1,0:T(8,128)(2,1)} %param.15) | copy-start | bytes 786436
  (18 other events, 28.8 us)
Sparse Core Ops, SparseCore 0:
  30.2 46.8 all-gather.4
  162.3 162.7 all-gather.6
  336.2 108.9 all-reduce.1
